TPU v7x, 512 devices: a whole 4x4x16 slice. The times are simulated.
512 devices in a mesh: dp: 8 (over y, x_lo), ctx: 64 (over z, x_hi, core).
Axes of the slice: x: 4 (x_hi: 2, x_lo: 2; x = x_hi * 2 + x_lo), y: 4, z: 16, core: 2. Of those that a mesh axis runs over, the one named last changes fastest.
Arguments:
- events: bfloat16 [8, 16384, 1024], P('dp', 'ctx'), may hold values from -6 to 6
- w_query: bfloat16 [1024, 512], replicated, may hold values from -0.1875 to 0.1875
- w_key: bfloat16 [1024, 512], replicated, may hold values from -0.1875 to 0.1875
- values: bfloat16 [8, 16384, 512], P('dp', 'ctx'), may hold values from -6 to 6
- grad_out: bfloat16 [8, 16384, 512], P('dp', 'ctx'), may hold values from -6 to 6
- lengths: int32 [8, 32], P('dp'), may hold values from 1 to 768, 16384 in all within a row
- stream_shift: int32 [8], P('dp'), may hold values from 0 to 16383
- block_keep: int32 [8, 128], P('dp'), may hold values 0 or 1
Outputs:
- attended: bfloat16 [8, 16384, 512], P('dp', 'ctx')
- grad_values: bfloat16 [8, 16384, 512], P('dp', 'ctx')
- grad_wq: bfloat16 [1024, 512], P('ctx')
- grad_wk: bfloat16 [1024, 512], P('ctx')
Inputs may be any that keep to these rules, and one draw needn't show every extreme that they name: The lengths of a stream sum to 16384; the longest is exactly 768.
All inputs are finite; a program needn't handle non-finite values. No bound on the sum of `block_keep` on one device may be relied on, other than what follows from the above.
Results may differ from a plain program's by a relative error of at most 0.011.
Values may be sent and summed in bfloat16 or wider, within the bound.
A program may use at most 64 MiB of HBM per device.

v0:
```python
import jax
import jax.numpy as jnp
from jax import lax
from jax.sharding import PartitionSpec as P

HD = 128
SPAN = 3
BLOCK = 128
MAXLEN = 768


def shifted(value, axis, steps):
    count = lax.axis_size(axis)
    pairs = [(source, (source + steps) % count) for source in range(count)]
    return lax.ppermute(value, axis, pairs)


def scores(query, key, valid, scale, alpha):
    z = jnp.einsum("qhd,khd->hqk", query, key, preferred_element_type=jnp.float32) * alpha
    sig = jax.nn.sigmoid(z)
    weight = valid[None, :, :].astype(jnp.float32) * scale
    return (z, sig, weight)


def forward_terms(query, grad, key, value, valid, scale, alpha):
    z, sig, weight = scores(query, key, valid, scale, alpha)
    att = (z * sig * weight).astype(jnp.bfloat16)
    out = jnp.einsum("hqk,khd->qhd", att, value, preferred_element_type=jnp.float32)
    dprod = jnp.einsum("qhd,khd->hqk", grad, value, preferred_element_type=jnp.float32)
    dsc = (dprod * sig * (1.0 + z * (1.0 - sig)) * weight * alpha).astype(jnp.bfloat16)
    dquery = jnp.einsum("hqk,khd->qhd", dsc, key, preferred_element_type=jnp.float32)
    return (out, dquery, att, dsc)


def backward_terms(query, grad, key, value, valid, scale, alpha):
    z, sig, weight = scores(query, key, valid, scale, alpha)
    att = (z * sig * weight).astype(jnp.bfloat16)
    dprod = jnp.einsum("qhd,khd->hqk", grad, value, preferred_element_type=jnp.float32)
    dsc = (dprod * sig * (1.0 + z * (1.0 - sig)) * weight * alpha).astype(jnp.bfloat16)
    dkey = jnp.einsum("hqk,qhd->khd", dsc, query, preferred_element_type=jnp.float32)
    dvalue = jnp.einsum("hqk,qhd->khd", att, grad, preferred_element_type=jnp.float32)
    return (dkey, dvalue)


def body(events, w_query, w_key, values, grad_out, lengths, stream_shift, block_keep):
    rows = events.shape[1]
    features = w_query.shape[1]
    nheads = features // HD
    alpha = 1.0 / HD**0.5
    scale = 1.0 / MAXLEN**0.5
    local = events[0]
    queries = jnp.dot(local, w_query, preferred_element_type=jnp.float32).astype(jnp.bfloat16)
    keys = jnp.dot(local, w_key, preferred_element_type=jnp.float32).astype(jnp.bfloat16)
    cycle_size = lax.axis_size("ctx")
    myself = lax.axis_index("ctx")
    total = rows * cycle_size
    ends = jnp.cumsum(lengths[0])
    offset = stream_shift[0]
    keep = block_keep[0]
    blocks_all = jnp.arange(keep.shape[0], dtype=jnp.int32)
    within = jnp.arange(rows, dtype=jnp.int32)

    def describe(anchor):
        anchor = jnp.remainder(anchor, cycle_size)
        position = jnp.remainder(anchor * rows + within - offset, total)
        owner = jnp.sum((position[:, None] >= ends[None, :]).astype(jnp.int32), axis=1)
        which = position // BLOCK
        kept = (
            jnp.sum(jnp.where(which[:, None] == blocks_all[None, :], keep[None, :], 0), axis=1) > 0
        )
        return (position, owner, kept)

    def mask(qinfo, kinfo):
        return (
            (qinfo[1][:, None] == kinfo[1][None, :])
            & (kinfo[0][None, :] <= qinfo[0][:, None])
            & kinfo[2][None, :]
        )

    def split(packed):
        return (
            packed[:, :features].reshape(rows, nheads, HD),
            packed[:, features:].reshape(rows, nheads, HD),
        )

    kv = jnp.concatenate([keys, values[0]], axis=1)
    qg = jnp.concatenate([queries, grad_out[0]], axis=1)
    kv_from = [None] + [shifted(kv, "ctx", step) for step in range(1, SPAN + 1)]
    qg_from = [None] + [shifted(qg, "ctx", -step) for step in range(1, SPAN + 1)]
    q_me, g_me = split(qg)
    k_me, v_me = split(kv)
    info_me = describe(myself)
    out_acc, dq_acc, att0, dsc0 = forward_terms(
        q_me, g_me, k_me, v_me, mask(info_me, info_me), scale, alpha
    )
    dk_acc = jnp.einsum("hqk,qhd->khd", dsc0, q_me, preferred_element_type=jnp.float32)
    dv_acc = jnp.einsum("hqk,qhd->khd", att0, g_me, preferred_element_type=jnp.float32)
    for step in range(1, SPAN + 1):
        k_s, v_s = split(kv_from[step])
        o, a, _, _ = forward_terms(
            q_me, g_me, k_s, v_s, mask(info_me, describe(myself - step)), scale, alpha
        )
        out_acc = out_acc + o
        dq_acc = dq_acc + a
        q_s, g_s = split(qg_from[step])
        b, c = backward_terms(
            q_s, g_s, k_me, v_me, mask(describe(myself + step), info_me), scale, alpha
        )
        dk_acc = dk_acc + b
        dv_acc = dv_acc + c
    attended = out_acc.reshape(1, rows, features).astype(jnp.bfloat16)
    grad_values = dv_acc.reshape(1, rows, features).astype(jnp.bfloat16)
    dq_b = dq_acc.reshape(rows, features).astype(jnp.bfloat16)
    dk_b = dk_acc.reshape(rows, features).astype(jnp.bfloat16)
    joined = jnp.concatenate([dq_b, dk_b], axis=1)
    terms = jnp.einsum("rd,rf->df", local, joined, preferred_element_type=jnp.float32)
    mine = lax.psum_scatter(terms, "ctx", scatter_dimension=0, tiled=True)
    mine = lax.psum(mine, "dp")
    grad_wq = mine[:, :features].astype(jnp.bfloat16)
    grad_wk = mine[:, features:].astype(jnp.bfloat16)
    return (attended, grad_values, grad_wq, grad_wk)


def solution(mesh):
    placed = (
        P("dp", "ctx", None),
        P(),
        P(),
        P("dp", "ctx", None),
        P("dp", "ctx", None),
        P("dp", None),
        P("dp"),
        P("dp", None),
    )
    return jax.shard_map(
        body,
        mesh=mesh,
        in_specs=placed,
        out_specs=(P("dp", "ctx", None), P("dp", "ctx", None), P("ctx", None), P("ctx", None)),
        check_vma=False,
    )
```

profile of v0, /device:TPU:4, one launch (start us, length us, event | category | flops | bytes accessed | tf_op | source)
XLA Modules:
  0.0 390.5 jit_solution(711006471729276778)
XLA Ops:
  7.3 1.2 copy-done
  8.5 1.5 convolution_convert_fusion.1
  10.0 1.0 pad_maximum_fusion.1
  11.0 10.8 %collective-permute-start.5 = (bf16[256,1024]{1,0:T(8,128)(2,1)S(1)}, bf16[256,1024]{1,0:T(8,128)(2,1)}, u32[]{:S(2)}, u32[]{:S(2)}) collective-permute-start(bf16[256,1024]{1,0:T(8,128)(2,1)S(1)} %pad_maximum_fusion.1), channel_id=1, source_target_pairs={{0,61},{1,62},{2,63},{3,0},{4,1},{5,2},{6,3},{7,4},{8,5},{9,6},{10... | collective-permute-start | bytes 1572872 | tf_op jit(solution)/shard_map/ppermute | solution.py:15
  21.8 2.4 collective-permute-start.4
  24.2 4.9 %collective-permute-start.3 = (bf16[256,1024]{1,0:T(8,128)(2,1)S(1)}, bf16[256,1024]{1,0:T(8,128)(2,1)}, u32[]{:S(2)}, u32[]{:S(2)}) collective-permute-start(bf16[256,1024]{1,0:T(8,128)(2,1)S(1)} %pad_maximum_fusion.1), channel_id=1, source_target_pairs={{0,63},{1,0},{2,1},{3,2},{4,3},{5,4},{6,5},{7,6},{8,7},{9,8},{10,9... | collective-permute-start | bytes 1572872 | tf_op jit(solution)/shard_map/ppermute | solution.py:15
  29.1 1.8 convolution_convert_fusion
  31.0 0.9 pad_maximum_fusion
  31.8 3.0 collective-permute-start.2
  34.8 4.8 %collective-permute-start.1 = (bf16[256,1024]{1,0:T(8,128)(2,1)}, bf16[256,1024]{1,0:T(8,128)(2,1)}, u32[]{:S(2)}, u32[]{:S(2)}) collective-permute-start(bf16[256,1024]{1,0:T(8,128)(2,1)} %pad_maximum_fusion), channel_id=1, source_target_pairs={{0,2},{1,3},{2,4},{3,5},{4,6},{5,7},{6,8},{7,9},{8,10},{9,11},{10,... | collective-permute-start | bytes 1572872 | tf_op jit(solution)/shard_map/ppermute | solution.py:15
  39.8 0.1 copy.196
  40.0 0.1 copy.195
  40.9 0.4 select_reduce_fusion.2
  41.5 0.1 reduce
  41.7 0.1 convert_reduce_fusion.2
  41.8 1.5 and_select_fusion.2
  43.3 0.6 multiply_convert_fusion.6
  43.9 0.6 fusion.30
  44.4 1.0 fusion.179
  45.5 1.1 fusion.178
  46.6 2.1 collective-permute-start
  48.7 1.8 slice_bitcast_fusion
  50.4 1.8 slice_bitcast_fusion.1
  52.3 1.8 slice_bitcast_fusion.2
  54.1 0.1 copy.202
  54.3 1.1 copy.201
  55.4 1.1 copy.200
  56.5 1.8 slice_bitcast_fusion.3
  58.3 1.8 copy.199
  60.1 6.7 %collective-permute-done.1 = bf16[256,1024]{1,0:T(8,128)(2,1)} collective-permute-done((bf16[256,1024]{1,0:T(8,128)(2,1)}, bf16[256,1024]{1,0:T(8,128)(2,1)}, u32[]{:S(2)}, u32[]{:S(2)}) %collective-permute-start.1) | collective-permute-done | bytes 524320 | tf_op jit(solution)/shard_map/ppermute | solution.py:15
  66.8 1.8 slice_bitcast_fusion.4
  68.7 1.8 copy.198
  70.5 1.8 slice_bitcast_fusion.5
  72.3 1.8 copy.197
  74.1 2.3 convolution_multiply_fusion.9
  76.4 2.3 convolution_multiply_fusion.8
  78.7 2.3 convolution_multiply_fusion.7
  81.0 1.4 convolution_multiply_fusion.6
  82.4 1.3 convolution_multiply_fusion.5
  83.7 1.3 convolution_multiply_fusion.4
  85.0 2.9 fusion.36
  87.9 2.9 fusion.35
  90.7 2.9 fusion.37
  93.7 2.9 fusion.42
  96.6 3.2 fusion.49
  99.8 3.2 fusion.52
  103.0 3.7 convolution_bitcast_fusion
  106.7 5.3 %copy.193 = f32[1024,1024]{1,0:T(8,128)} copy(f32[1024,1024]{0,1:T(8,128)} %convolution_bitcast_fusion) | data formatting | bytes 8388608
  112.1 0.3 convolution_bitcast_fusion.4
  112.3 0.3 convolution_bitcast_fusion.11
  112.7 0.3 copy-done.18
  113.1 1.8 convolution_bitcast_fusion.8
  114.9 0.5 convolution_bitcast_fusion.9
  115.4 0.5 fusion.51
  115.9 0.8 copy.186
  116.7 1.9 convolution_bitcast_fusion.5
  118.7 1.4 convolution_bitcast_fusion.6
  120.1 0.5 fusion.50
  120.6 0.8 copy.187
  121.5 217.4 %reduce-scatter.4.cloned.1.call-done = f32[16,1024]{1,0:T(8,128)} async-done(((f32[1024,1024]{1,0:T(8,128)}), f32[16,1024]{1,0:T(8,128)}) %reduce-scatter.4.cloned.1.call-update) | async-done | bytes 65552
  338.8 1.0 copy.194
  339.9 42.3 %psum.7 = bf16[16,1024]{0,1:T(8,128)(2,1)S(1)} all-reduce(f32[16,1024]{0,1:T(8,128)S(1)} %copy.194), channel_id=1, replica_groups=mesh['dp'=8,'ctx'=64] {'dp'}, use_global_device_ids=true, to_apply=%region_13.14 | all-reduce | flops 16384 | bytes 98304 | tf_op jit(solution)/shard_map/psum | solution.py:118
  382.2 0.7 copy.189
  382.9 0.7 copy.188
  (70 shorter events, 0.7 us)
Async XLA Ops:
  7.2 1.3 copy-start
  7.2 32.6 %copy-start.7 = (bf16[1,256,512]{2,1,0:T(8,128)(2,1)S(1)}, bf16[1,256,512]{2,1,0:T(8,128)(2,1)}, u32[]{:S(2)}) copy-start(bf16[1,256,512]{2,1,0:T(8,128)(2,1)} %param.12) | copy-start | bytes 786436
  7.2 23.8 %copy-start.6 = (bf16[1,256,512]{2,1,0:T(8,128)(2,1)S(1)}, bf16[1,256,512]{2,1,0:T(8,128)(2,1)}, u32[]{:S(2)}) copy-start(bf16[1,256,512]{2,1,0:T(8,128)(2,1)} %param.11) | copy-start | bytes 786436
  7.2 33.7 %copy-start.23 = (s32[1,128]{1,0:T(1,128)S(1)}, s32[1,128]{1,0:T(1,128)}, u32[]{:S(2)}) copy-start(s32[1,128]{1,0:T(1,128)} %param.15) | copy-start | bytes 1540
  7.2 34.2 %copy-start.24 = (s32[1,32]{1,0:T(1,128)S(1)}, s32[1,32]{1,0:T(1,128)}, u32[]{:S(2)}) copy-start(s32[1,32]{1,0:T(1,128)} %param.13) | copy-start | bytes 388
  7.2 331.6 %reduce-scatter.4.cloned.1.call-start = ((), (), s32[]{:S(2)}) async-start(), calls=%async_computation.1 | async-start | bytes 4259840
  11.0 35.6 %collective-permute-start.5 = (bf16[256,1024]{1,0:T(8,128)(2,1)S(1)}, bf16[256,1024]{1,0:T(8,128)(2,1)}, u32[]{:S(2)}, u32[]{:S(2)}) collective-permute-start(bf16[256,1024]{1,0:T(8,128)(2,1)S(1)} %pad_maximum_fusion.1), channel_id=1, source_target_pairs={{0,61},{1,62},{2,63},{3,0},{4,1},{5,2},{6,3},{7,4},{8,5},{9,6},{10... | collective-permute-start | bytes 1572872 | tf_op jit(solution)/shard_map/ppermute | solution.py:15
  21.8 28.6 %collective-permute-start.4 = (bf16[256,1024]{1,0:T(8,128)(2,1)S(1)}, bf16[256,1024]{1,0:T(8,128)(2,1)}, u32[]{:S(2)}, u32[]{:S(2)}) collective-permute-start(bf16[256,1024]{1,0:T(8,128)(2,1)S(1)} %pad_maximum_fusion.1), channel_id=1, source_target_pairs={{0,62},{1,63},{2,0},{3,1},{4,2},{5,3},{6,4},{7,5},{8,6},{9,7},{10,... | collective-permute-start | bytes 1572872 | tf_op jit(solution)/shard_map/ppermute | solution.py:15
  24.2 28.0 %collective-permute-start.3 = (bf16[256,1024]{1,0:T(8,128)(2,1)S(1)}, bf16[256,1024]{1,0:T(8,128)(2,1)}, u32[]{:S(2)}, u32[]{:S(2)}) collective-permute-start(bf16[256,1024]{1,0:T(8,128)(2,1)S(1)} %pad_maximum_fusion.1), channel_id=1, source_target_pairs={{0,63},{1,0},{2,1},{3,2},{4,3},{5,4},{6,5},{7,6},{8,7},{9,8},{10,9... | collective-permute-start | bytes 1572872 | tf_op jit(solution)/shard_map/ppermute | solution.py:15
  31.8 24.6 %collective-permute-start.2 = (bf16[256,1024]{1,0:T(8,128)(2,1)}, bf16[256,1024]{1,0:T(8,128)(2,1)}, u32[]{:S(2)}, u32[]{:S(2)}) collective-permute-start(bf16[256,1024]{1,0:T(8,128)(2,1)} %pad_maximum_fusion), channel_id=1, source_target_pairs={{0,3},{1,4},{2,5},{3,6},{4,7},{5,8},{6,9},{7,10},{8,11},{9,12},{10... | collective-permute-start | bytes 1572872 | tf_op jit(solution)/shard_map/ppermute | solution.py:15
  34.8 32.0 %collective-permute-start.1 = (bf16[256,1024]{1,0:T(8,128)(2,1)}, bf16[256,1024]{1,0:T(8,128)(2,1)}, u32[]{:S(2)}, u32[]{:S(2)}) collective-permute-start(bf16[256,1024]{1,0:T(8,128)(2,1)} %pad_maximum_fusion), channel_id=1, source_target_pairs={{0,2},{1,3},{2,4},{3,5},{4,6},{5,7},{6,8},{7,9},{8,10},{9,11},{10,... | collective-permute-start | bytes 1572872 | tf_op jit(solution)/shard_map/ppermute | solution.py:15
  46.6 23.9 %collective-permute-start = (bf16[256,1024]{1,0:T(8,128)(2,1)}, bf16[256,1024]{1,0:T(8,128)(2,1)}, u32[]{:S(2)}, u32[]{:S(2)}) collective-permute-start(bf16[256,1024]{1,0:T(8,128)(2,1)} %pad_maximum_fusion), channel_id=1, source_target_pairs={{0,1},{1,2},{2,3},{3,4},{4,5},{5,6},{6,7},{7,8},{8,9},{9,10},{10,1... | collective-permute-start | bytes 1572872 | tf_op jit(solution)/shard_map/ppermute | solution.py:15
  83.7 4.2 %copy-start.14 = (f32[256,256]{1,0:T(8,128)S(1)}, f32[256,256]{1,0:T(8,128)}, u32[]{:S(2)}) copy-start(f32[256,256]{1,0:T(8,128)} %get-tuple-element.47) | copy-start | bytes 786436
  87.9 2.9 copy-start.8
  90.7 3.0 copy-start.10
  90.7 3.0 copy-start.12
  93.7 2.9 copy-start.9
  96.6 3.2 copy-start.11
  99.8 3.2 copy-start.1
  112.0 0.9 copy-start.18
  112.0 1.0 copy-start.20
  112.0 2.8 copy-start.5
  112.1 2.8 copy-start.17
  112.1 2.8 copy-start.21
  113.0 2.3 copy-start.4
  113.0 2.3 copy-start.16
  113.0 2.3 copy-start.22
  115.8 2.8 copy-start.3
  115.8 2.8 copy-start.15
  116.7 3.4 copy-start.2
  116.7 3.4 copy-start.13
  116.7 3.4 copy-start.19
Sparse Core Ops, SparseCore 0:
  112.2 226.6 reduce-scatter.3
where the time goes:
time: 392 us; the launch traced here: 390 us
  waiting for transfers between devices  224 us (57%)
  matrix products  46.2 us (12%)
  blocking collectives  42.3 us (11%)
  local copies, waits for them, and re-layouts  30.3 us (8%)
  starting transfers between devices  28 us (7%)
  between operations  15.3 us (4%)
  other arithmetic  4.22 us (1%)
    unnamed x2, waiting for transfers between devices  217 us
    psum x1, blocking collectives, body(): mine = lax.psum(mine, 'dp')  42.3 us
    ppermute x6, starting transfers between devices, shifted(): return lax.ppermute(value, axis, pairs)  28 us
    unnamed x62, local copies, waits for them, and re-layouts  22.1 us
    dot_general x7, matrix products, scores(): jnp.einsum('qhd,khd->hqk', query, key, preferred_element_type=jnp.float32)  11.5 us
    dot_general x4, matrix products, forward_terms(): jnp.einsum('hqk,khd->qhd', dsc, key, preferred_element_type=jnp.float32)  10.1 us
    dot_general x3, matrix products, backward_terms(): jnp.einsum('hqk,qhd->khd', dsc, query, preferred_element_type=jnp.float32)  8.86 us
    reshape x8, local copies, waits for them, and re-layouts, split(): packed[:, :features].reshape(rows, nheads, HD)  7.94 us
  transfers between devices with their start and end apart: 7, of which 2 were waited for; matrix products, arithmetic and copies ran while one was open for 8% of the time, Pallas kernels for 0%

commit v1 on v0

--- a/solution.py
+++ b/solution.py
@@ -115,7 +115,7 @@
     joined = jnp.concatenate([dq_b, dk_b], axis=1)
     terms = jnp.einsum("rd,rf->df", local, joined, preferred_element_type=jnp.float32)
     mine = lax.psum_scatter(terms, "ctx", scatter_dimension=0, tiled=True)
-    mine = lax.psum(mine, "dp")
+    mine = jnp.sum(lax.all_gather(mine, "dp"), axis=0)
     grad_wq = mine[:, :features].astype(jnp.bfloat16)
     grad_wk = mine[:, features:].astype(jnp.bfloat16)
     return (attended, grad_values, grad_wq, grad_wk)

time: 392 us -> 378 us (0.964)
  the two profiles are of different devices: /device:TPU:4 before, /device:TPU:2 now
where the time goes in v1:
time: 378 us; the launch traced here: 377 us
  waiting for transfers between devices  226 us (60%)
  matrix products  45.8 us (12%)
  blocking collectives  29.8 us (8%)
  local copies, waits for them, and re-layouts  28.1 us (7%)
  starting transfers between devices  27.3 us (7%)
  between operations  15.4 us (4%)
  other arithmetic  4.24 us (1%)
    reduce_scatter x1, waiting for transfers between devices, body(): mine = lax.psum_scatter(terms, 'ctx', scatter_dimension=0, tiled=True)  219 us
    all_gather x1, blocking collectives, body(): mine = jnp.sum(lax.all_gather(mine, 'dp'), axis=0)  29.8 us
    ppermute x6, starting transfers between devices, shifted(): return lax.ppermute(value, axis, pairs)  27.2 us
    unnamed x65, local copies, waits for them, and re-layouts  19.3 us
    dot_general x7, matrix products, scores(): jnp.einsum('qhd,khd->hqk', query, key, preferred_element_type=jnp.float32)  11.5 us
    dot_general x4, matrix products, forward_terms(): jnp.einsum('hqk,khd->qhd', dsc, key, preferred_element_type=jnp.float32)  10.1 us
    dot_general x3, matrix products, backward_terms(): jnp.einsum('hqk,qhd->khd', dsc, query, preferred_element_type=jnp.float32)  8.85 us
    reshape x8, local copies, waits for them, and re-layouts, split(): packed[:, :features].reshape(rows, nheads, HD)  7.94 us
  transfers between devices with their start and end apart: 7, of which 2 were waited for; matrix products, arithmetic and copies ran while one was open for 9% of the time, Pallas kernels for 0%

profile of v1, /device:TPU:2, one launch (start us, length us, event | category | flops | bytes accessed | tf_op | source)
XLA Modules:
  0.0 376.5 jit_solution(8356875037157081708)
XLA Ops:
  7.3 1.2 copy-done
  8.5 1.5 convolution_convert_fusion.1
  10.0 1.0 pad_maximum_fusion.1
  11.0 10.8 %collective-permute-start.5 = (bf16[256,1024]{1,0:T(8,128)(2,1)S(1)}, bf16[256,1024]{1,0:T(8,128)(2,1)}, u32[]{:S(2)}, u32[]{:S(2)}) collective-permute-start(bf16[256,1024]{1,0:T(8,128)(2,1)S(1)} %pad_maximum_fusion.1), channel_id=1, source_target_pairs={{0,61},{1,62},{2,63},{3,0},{4,1},{5,2},{6,3},{7,4},{8,5},{9,6},{10... | collective-permute-start | bytes 1572872 | tf_op jit(solution)/shard_map/ppermute | solution.py:15
  21.8 4.5 %collective-permute-start.4 = (bf16[256,1024]{1,0:T(8,128)(2,1)S(1)}, bf16[256,1024]{1,0:T(8,128)(2,1)}, u32[]{:S(2)}, u32[]{:S(2)}) collective-permute-start(bf16[256,1024]{1,0:T(8,128)(2,1)S(1)} %pad_maximum_fusion.1), channel_id=1, source_target_pairs={{0,62},{1,63},{2,0},{3,1},{4,2},{5,3},{6,4},{7,5},{8,6},{9,7},{10,... | collective-permute-start | bytes 1572872 | tf_op jit(solution)/shard_map/ppermute | solution.py:15
  26.3 4.9 %collective-permute-start.3 = (bf16[256,1024]{1,0:T(8,128)(2,1)S(1)}, bf16[256,1024]{1,0:T(8,128)(2,1)}, u32[]{:S(2)}, u32[]{:S(2)}) collective-permute-start(bf16[256,1024]{1,0:T(8,128)(2,1)S(1)} %pad_maximum_fusion.1), channel_id=1, source_target_pairs={{0,63},{1,0},{2,1},{3,2},{4,3},{5,4},{6,5},{7,6},{8,7},{9,8},{10,9... | collective-permute-start | bytes 1572872 | tf_op jit(solution)/shard_map/ppermute | solution.py:15
  31.2 1.8 convolution_convert_fusion
  33.0 0.9 pad_maximum_fusion
  33.9 1.9 collective-permute-start.2
  35.8 3.0 collective-permute-start.1
  38.9 0.1 reshape_squeeze.6
  39.0 0.1 reshape_squeeze.7
  39.1 0.1 copy.191
  39.2 0.1 copy.190
  40.2 0.4 select_reduce_fusion.2
  40.7 0.1 copy.136
  40.8 0.1 reduce
  40.9 0.1 convert_reduce_fusion.2
  41.1 1.5 and_select_fusion.2
  42.6 0.6 multiply_convert_fusion.6
  43.1 0.6 fusion.30
  43.7 1.0 fusion.179
  44.7 1.1 fusion.178
  45.9 2.1 collective-permute-start
  48.0 1.8 slice_bitcast_fusion
  49.7 1.8 slice_bitcast_fusion.1
  51.6 1.8 slice_bitcast_fusion.2
  53.4 0.1 copy.197
  53.5 1.1 copy.196
  54.6 1.1 copy.195
  55.7 1.8 slice_bitcast_fusion.3
  57.6 1.8 copy.194
  59.4 6.5 %collective-permute-done.1 = bf16[256,1024]{1,0:T(8,128)(2,1)} collective-permute-done((bf16[256,1024]{1,0:T(8,128)(2,1)}, bf16[256,1024]{1,0:T(8,128)(2,1)}, u32[]{:S(2)}, u32[]{:S(2)}) %collective-permute-start.1) | collective-permute-done | bytes 524320 | tf_op jit(solution)/shard_map/ppermute | solution.py:15
  65.9 1.8 slice_bitcast_fusion.4
  67.7 1.8 copy.193
  69.5 1.8 slice_bitcast_fusion.5
  71.4 1.8 copy.192
  73.2 2.3 convolution_multiply_fusion.9
  75.4 2.3 convolution_multiply_fusion.8
  77.8 2.3 convolution_multiply_fusion.7
  80.0 1.4 convolution_multiply_fusion.6
  81.4 1.3 convolution_multiply_fusion.5
  82.7 1.3 convolution_multiply_fusion.4
  84.1 2.9 fusion.36
  87.0 2.8 fusion.35
  89.8 3.0 fusion.37
  92.8 2.9 fusion.42
  95.7 3.2 fusion.49
  98.9 3.1 fusion.52
  102.0 3.7 convolution_bitcast_fusion
  105.7 5.3 %copy.188 = f32[1024,1024]{1,0:T(8,128)} copy(f32[1024,1024]{0,1:T(8,128)} %convolution_bitcast_fusion) | data formatting | bytes 8388608
  111.1 1.1 convolution_bitcast_fusion.4
  112.2 0.3 convolution_bitcast_fusion.11
  112.6 1.8 convolution_bitcast_fusion.8
  114.4 0.5 convolution_bitcast_fusion.9
  114.9 0.5 fusion.51
  115.4 0.8 copy.183
  116.3 1.6 convolution_bitcast_fusion.5
  118.0 0.5 convolution_bitcast_fusion.6
  118.5 0.5 fusion.50
  119.0 0.8 copy.184
  119.8 219.4 %reduce-scatter.4.cloned.1.call-done = f32[16,1024]{1,0:T(8,128)} async-done(((f32[1024,1024]{1,0:T(8,128)}), f32[16,1024]{1,0:T(8,128)}) %reduce-scatter.4.cloned.1.call-update) | async-done | bytes 65552 | tf_op jit(solution)/shard_map/reduce_scatter | solution.py:117
  339.3 29.8 %all-gather = f32[128,1024]{1,0:T(8,128)S(1)} all-gather(f32[16,1024]{1,0:T(8,128)} %reduce-scatter.4.cloned.1.call-done), channel_id=2, replica_groups=mesh['dp'=8,'ctx'=64] {'dp'}, dimensions={0}, use_global_device_ids=true | all-gather | bytes 589824 | tf_op jit(solution)/shard_map/all_gather | solution.py:118
  369.1 0.6 fusion.177
  (74 shorter events, 0.4 us)
Async XLA Ops:
  7.2 1.3 copy-start
  7.2 31.8 %copy-start.8 = (bf16[1,256,512]{2,1,0:T(8,128)(2,1)S(1)}, bf16[1,256,512]{2,1,0:T(8,128)(2,1)}, u32[]{:S(2)}) copy-start(bf16[1,256,512]{2,1,0:T(8,128)(2,1)} %param.12) | copy-start | bytes 786436
  7.2 25.8 %copy-start.7 = (bf16[1,256,512]{2,1,0:T(8,128)(2,1)S(1)}, bf16[1,256,512]{2,1,0:T(8,128)(2,1)}, u32[]{:S(2)}) copy-start(bf16[1,256,512]{2,1,0:T(8,128)(2,1)} %param.11) | copy-start | bytes 786436
  7.2 33.0 %copy-start.26 = (s32[1,128]{1,0:T(1,128)S(1)}, s32[1,128]{1,0:T(1,128)}, u32[]{:S(2)}) copy-start(s32[1,128]{1,0:T(1,128)} %param.15) | copy-start | bytes 1540
  7.2 33.4 %copy-start.27 = (s32[1,32]{1,0:T(1,128)S(1)}, s32[1,32]{1,0:T(1,128)}, u32[]{:S(2)}) copy-start(s32[1,32]{1,0:T(1,128)} %param.13) | copy-start | bytes 388
  7.2 332.0 %reduce-scatter.4.cloned.1.call-start = ((), (), s32[]{:S(2)}) async-start(), calls=%async_computation.1 | async-start | bytes 4259840 | tf_op jit(solution)/shard_map/reduce_scatter | solution.py:117
  11.0 34.9 %collective-permute-start.5 = (bf16[256,1024]{1,0:T(8,128)(2,1)S(1)}, bf16[256,1024]{1,0:T(8,128)(2,1)}, u32[]{:S(2)}, u32[]{:S(2)}) collective-permute-start(bf16[256,1024]{1,0:T(8,128)(2,1)S(1)} %pad_maximum_fusion.1), channel_id=1, source_target_pairs={{0,61},{1,62},{2,63},{3,0},{4,1},{5,2},{6,3},{7,4},{8,5},{9,6},{10... | collective-permute-start | bytes 1572872 | tf_op jit(solution)/shard_map/ppermute | solution.py:15
  21.8 27.9 %collective-permute-start.4 = (bf16[256,1024]{1,0:T(8,128)(2,1)S(1)}, bf16[256,1024]{1,0:T(8,128)(2,1)}, u32[]{:S(2)}, u32[]{:S(2)}) collective-permute-start(bf16[256,1024]{1,0:T(8,128)(2,1)S(1)} %pad_maximum_fusion.1), channel_id=1, source_target_pairs={{0,62},{1,63},{2,0},{3,1},{4,2},{5,3},{6,4},{7,5},{8,6},{9,7},{10,... | collective-permute-start | bytes 1572872 | tf_op jit(solution)/shard_map/ppermute | solution.py:15
  26.3 25.3 %collective-permute-start.3 = (bf16[256,1024]{1,0:T(8,128)(2,1)S(1)}, bf16[256,1024]{1,0:T(8,128)(2,1)}, u32[]{:S(2)}, u32[]{:S(2)}) collective-permute-start(bf16[256,1024]{1,0:T(8,128)(2,1)S(1)} %pad_maximum_fusion.1), channel_id=1, source_target_pairs={{0,63},{1,0},{2,1},{3,2},{4,3},{5,4},{6,5},{7,6},{8,7},{9,8},{10,9... | collective-permute-start | bytes 1572872 | tf_op jit(solution)/shard_map/ppermute | solution.py:15
  33.9 21.8 %collective-permute-start.2 = (bf16[256,1024]{1,0:T(8,128)(2,1)}, bf16[256,1024]{1,0:T(8,128)(2,1)}, u32[]{:S(2)}, u32[]{:S(2)}) collective-permute-start(bf16[256,1024]{1,0:T(8,128)(2,1)} %pad_maximum_fusion), channel_id=1, source_target_pairs={{0,3},{1,4},{2,5},{3,6},{4,7},{5,8},{6,9},{7,10},{8,11},{9,12},{10... | collective-permute-start | bytes 1572872 | tf_op jit(solution)/shard_map/ppermute | solution.py:15
  35.8 30.1 %collective-permute-start.1 = (bf16[256,1024]{1,0:T(8,128)(2,1)}, bf16[256,1024]{1,0:T(8,128)(2,1)}, u32[]{:S(2)}, u32[]{:S(2)}) collective-permute-start(bf16[256,1024]{1,0:T(8,128)(2,1)} %pad_maximum_fusion), channel_id=1, source_target_pairs={{0,2},{1,3},{2,4},{3,5},{4,6},{5,7},{6,8},{7,9},{8,10},{9,11},{10,... | collective-permute-start | bytes 1572872 | tf_op jit(solution)/shard_map/ppermute | solution.py:15
  45.9 23.7 %collective-permute-start = (bf16[256,1024]{1,0:T(8,128)(2,1)}, bf16[256,1024]{1,0:T(8,128)(2,1)}, u32[]{:S(2)}, u32[]{:S(2)}) collective-permute-start(bf16[256,1024]{1,0:T(8,128)(2,1)} %pad_maximum_fusion), channel_id=1, source_target_pairs={{0,1},{1,2},{2,3},{3,4},{4,5},{5,6},{6,7},{7,8},{8,9},{9,10},{10,1... | collective-permute-start | bytes 1572872 | tf_op jit(solution)/shard_map/ppermute | solution.py:15
  82.7 4.2 %copy-start.16 = (f32[256,256]{1,0:T(8,128)S(1)}, f32[256,256]{1,0:T(8,128)}, u32[]{:S(2)}) copy-start(f32[256,256]{1,0:T(8,128)} %get-tuple-element.47) | copy-start | bytes 786436
  86.9 2.9 copy-start.9
  89.8 3.0 copy-start.11
  89.8 3.0 copy-start.13
  92.8 2.9 copy-start.10
  95.7 3.2 copy-start.12
  98.9 3.2 copy-start.1
  111.1 1.5 copy-start.20
  111.1 1.5 copy-start.23
  111.1 3.3 copy-start.6
  111.1 3.3 copy-start.19
  111.1 3.3 copy-start.24
  112.6 2.3 copy-start.5
  112.6 2.3 copy-start.18
  112.6 2.3 copy-start.25
  114.9 1.3 copy-start.4
  115.4 2.6 copy-start.3
  116.2 1.7 copy-start.17
  116.2 1.7 copy-start.21
  116.3 2.2 copy-start.2
  116.3 2.2 copy-start.14
  116.3 2.2 copy-start.15
  116.3 2.2 copy-start.22
Sparse Core Ops, SparseCore 0:
  111.2 227.9 reduce-scatter.3
